TPU v7x, 32 devices: a whole 2x2x4 slice. The times are simulated.
32 devices in a mesh: seg: 4 (over y, x), bin: 8 (over z, core).
Axes of the slice: x: 2, y: 2, z: 4, core: 2. Of those that a mesh axis runs over, the one named last changes fastest.
Arguments:
- coverage_lanes: bfloat16 [256, 128, 128], P(('seg', 'bin')), may hold values from 4 to 64
- target_blocks: int32 [256], P(('seg', 'bin')), may hold values from 0 to 7, as said below
- valid_bins: int32 [256], P(('seg', 'bin')), may hold values from 1 to 128
- panel_mean: float32 [32768], P(('seg', 'bin')), may hold values from 3.5 to 5
- components: float32 [256, 32768], P(None, ('seg', 'bin')), as said below
- kernels: float32 [3, 33, 32768], P(None, None, ('seg', 'bin')), may hold values from 0 to 0.08
- chrom_starts: int32 [24], replicated, may hold values from 0 to 32767, as said below
Outputs:
- coefficients: float32 [128, 256], replicated
- smoothed: float32 [128, 32768], P(None, ('seg', 'bin'))
- bridge: float32 [128, 32768], P(None, ('seg', 'bin'))
Inputs may be any that keep to these rules, and one draw needn't show every extreme that they name: target_blocks names one of the owner's 8 blocks; slot r of a device goes to the owner given by r // 1 within the device's stretch. `chrom_starts`: strictly rising chromosome starts, the first is 0 and the last is 32767. panel-of-normals components.
All inputs are finite; a program needn't handle non-finite values.
Results may differ from a plain program's by a relative error of at most 0.0003.
Values may be sent and summed in bfloat16 or wider, within the bound.
A program may use at most 192 MiB of HBM per device.

v0:
```python
import math
import jax
import jax.numpy as jnp
from jax import lax
from jax.sharding import PartitionSpec as P


def extended(block, sides, width):
    for axis, dim in sides:
        count = lax.axis_size(axis)
        forward = [(i, i + 1) for i in range(count - 1)]
        backward = [(target, source) for source, target in forward]
        low = lax.ppermute(
            lax.slice_in_dim(block, block.shape[dim] - width, None, axis=dim), axis, forward
        )
        high = lax.ppermute(lax.slice_in_dim(block, 0, width, axis=dim), axis, backward)
        block = jnp.concatenate([low, block, high], axis=dim)
    return block


def prefix(part, axis, combine, identity):
    place = lax.axis_index(axis)
    gathered = lax.all_gather(part, axis)
    state = jnp.zeros_like(part) + jnp.asarray(identity, part.dtype)

    def one(hop, state):
        return combine(state, lax.dynamic_index_in_dim(gathered, hop, 0, False))

    return lax.fori_loop(0, place, one, state)


def chrom_labels(chrom_starts, first_bin, count, total_bins):
    positions = first_bin + lax.iota(jnp.int32, count)
    covered = jnp.sum((chrom_starts[:, None] <= positions[None, :]).astype(jnp.int32), axis=0) - 1
    return jnp.where(positions >= total_bins, chrom_starts.shape[0], covered)


def smooth_once(padded, tap_weights, labels, out_width):
    half_taps = (tap_weights.shape[0] - 1) // 2
    centre = labels[half_taps : half_taps + out_width]
    result = jnp.zeros((padded.shape[0], out_width), jnp.float32)
    for tap_index in range(tap_weights.shape[0]):
        weight = tap_weights[tap_index] * (
            labels[tap_index : tap_index + out_width] == centre
        ).astype(jnp.float32)
        result = result + weight[None, :] * padded[:, tap_index : tap_index + out_width]
    return result


def add_terms(earlier, later):
    return earlier + later


def per_device(
    coverage_lanes, target_blocks, valid_bins, panel_mean, components, kernels, chrom_starts
):
    slot_count, samples, block_bins = coverage_lanes.shape
    bin_dev = panel_mean.shape[0]
    blocks_dev = bin_dev // block_bins
    total_bins = bin_dev * lax.axis_size(("seg", "bin"))
    first_bin = lax.axis_index(("seg", "bin")) * bin_dev
    keep_mask = (lax.iota(jnp.int32, block_bins)[None, :] < valid_bins[:, None]).astype(
        jnp.bfloat16
    )
    masked = coverage_lanes * keep_mask[:, None, :]
    arrived, arrived_targets = (
        lax.all_to_all(masked, "bin", split_axis=0, concat_axis=0, tiled=True),
        lax.all_to_all(
            target_blocks.astype(jnp.bfloat16), "bin", split_axis=0, concat_axis=0, tiled=True
        ),
    )
    block_names = lax.iota(jnp.int32, blocks_dev).astype(jnp.bfloat16)
    placing = (arrived_targets[None, :] == block_names[:, None]).astype(jnp.bfloat16)
    coverage = jnp.einsum("br,rsc->sbc", placing, arrived, preferred_element_type=jnp.float32)
    coverage = coverage.reshape(samples, bin_dev)
    log_ratio = jnp.log(coverage + 1.0) - panel_mean[None, :]
    partial_terms = lax.dot_general(
        log_ratio,
        components,
        (((1,), (1,)), ((), ())),
        precision=lax.Precision.HIGHEST,
        preferred_element_type=jnp.float32,
    )
    coefficients = lax.psum(partial_terms, ("seg", "bin"))
    signal = log_ratio - jnp.dot(
        coefficients,
        components,
        precision=lax.Precision.HIGHEST,
        preferred_element_type=jnp.float32,
    )
    layers = kernels.shape[0]
    half_taps = (kernels.shape[1] - 1) // 2
    labels = chrom_labels(chrom_starts, first_bin - half_taps, bin_dev + 2 * half_taps, total_bins)
    smoothed = signal
    for layer_index in range(layers):
        padded = extended(smoothed, ((("seg", "bin"), 1),), half_taps)
        smoothed = smooth_once(padded, kernels[layer_index], labels, bin_dev)
    totals = lax.psum(jnp.sum(smoothed, axis=1), ("seg", "bin"))
    centred = smoothed - (totals / total_bins)[:, None]
    blocks_view = centred.reshape(samples, blocks_dev, block_bins)
    upper_ones = (
        lax.iota(jnp.int32, block_bins)[:, None] <= lax.iota(jnp.int32, block_bins)[None, :]
    ).astype(jnp.float32)
    inside = jnp.einsum(
        "snc,cd->snd",
        blocks_view,
        upper_ones,
        precision=lax.Precision.HIGHEST,
        preferred_element_type=jnp.float32,
    )
    block_sums = inside[:, :, -1]
    running = jnp.cumsum(block_sums, axis=1)
    local_prefix = inside + (running - block_sums)[:, :, None]
    local_total = running[:, -1]
    zero_terms = jnp.zeros_like(local_total)
    before = prefix(local_total, ("seg", "bin"), add_terms, zero_terms)
    bridge = (local_prefix.reshape(samples, bin_dev) + before[:, None]) * (
        1.0 / math.sqrt(total_bins)
    )
    return (coefficients, smoothed, bridge)


def solution(mesh):
    in_specs = (
        P(("seg", "bin"), None, None),
        P(("seg", "bin")),
        P(("seg", "bin")),
        P(("seg", "bin")),
        P(None, ("seg", "bin")),
        P(None, None, ("seg", "bin")),
        P(),
    )
    out_specs = (P(), P(None, ("seg", "bin")), P(None, ("seg", "bin")))
    return jax.shard_map(
        per_device, mesh=mesh, in_specs=in_specs, out_specs=out_specs, check_vma=False
    )
```

profile of v0, /device:TPU:5, one launch (start us, length us, event | category | flops | bytes accessed | tf_op | source)
XLA Modules:
  0.0 307.1 jit_solution(12977762061642653183)
XLA Ops:
  7.2 0.7 convert_bitcast_fusion
  7.9 0.7 copy.21
  8.6 5.5 %all-to-all-start.1 = ((bf16[8,1,1]{2,1,0:T(2,128)(2,1)}), bf16[8,1,1]{2,1,0:T(2,128)(2,1)S(1)}, u32[]{:S(2)}, u32[]{:S(2)}) async-start(bf16[8,1,1]{2,1,0:T(2,128)(2,1)} %copy.21), calls=%async_computation.1 | async-start | bytes 8192 | tf_op jit(solution)/shard_map/all_to_all | solution.py:68
  14.2 0.8 fusion.306
  15.0 1.4 fusion.303
  16.4 1.4 fusion.305
  17.8 1.4 fusion.302
  19.1 1.4 fusion.301
  20.5 1.7 fusion.304
  22.2 0.6 copy-done.5
  22.9 0.6 copy-done.6
  23.6 0.1 convert_reduce_fusion
  23.7 0.7 broadcast_multiply_fusion
  24.5 0.1 broadcast_select_fusion.27
  24.6 0.1 broadcast_select_fusion.95
  24.6 0.1 broadcast_select_fusion.28
  24.8 0.1 broadcast_select_fusion.30
  24.8 0.1 broadcast_select_fusion.29
  25.1 5.1 %all-to-all-start = ((bf16[8,128,128]{2,1,0:T(8,128)(2,1)}), bf16[8,128,128]{2,1,0:T(8,128)(2,1)S(1)}, u32[]{:S(2)}, u32[]{:S(2)}) async-start(bf16[8,128,128]{2,1,0:T(8,128)(2,1)} %broadcast_multiply_fusion), calls=%async_computation | async-start | bytes 524288 | tf_op jit(solution)/shard_map/all_to_all | solution.py:67
  30.2 0.1 reduce
  30.4 8.5 %all-to-all-done = bf16[8,128,128]{2,1,0:T(8,128)(2,1)S(1)} async-done(((bf16[8,128,128]{2,1,0:T(8,128)(2,1)}), bf16[8,128,128]{2,1,0:T(8,128)(2,1)S(1)}, u32[]{:S(2)}, u32[]{:S(2)}) %all-to-all-start) | async-done | bytes 262176 | tf_op jit(solution)/shard_map/all_to_all | solution.py:67
  38.9 0.3 fusion
  39.2 0.4 copy-done.4
  39.6 1.8 fusion.286
  41.5 121.1 %all-reduce.2.cloned.1.call-done = f32[128,256]{1,0:T(8,128)} async-done(((f32[128,256]{1,0:T(8,128)}), f32[128,256]{1,0:T(8,128)}) %all-reduce.2.cloned.1.call-update) | async-done | bytes 131088 | tf_op jit(solution)/shard_map/psum | solution.py:84
  162.5 1.7 convolution_subtract_fusion
  164.2 0.1 fusion.300
  164.3 4.3 %collective-permute-start = (f32[128,16]{1,0:T(8,128)S(1)}, f32[128,16]{1,0:T(8,128)S(1)}, u32[]{:S(2)}, u32[]{:S(2)}) collective-permute-start(f32[128,16]{1,0:T(8,128)S(1)} %get-tuple-element.105), channel_id=1, source_target_pairs={{0,1},{1,2},{2,3},{3,4},{4,5},{5,6},{6,7},{7,8},{8,9},{9,10},{10,1... | collective-permute-start | bytes 24584 | tf_op jit(solution)/shard_map/ppermute | solution.py:13
  168.6 1.9 collective-permute-start.1
  170.6 3.9 %collective-permute-done.1 = f32[128,16]{1,0:T(8,128)S(1)} collective-permute-done((f32[128,16]{1,0:T(8,128)S(1)}, f32[128,16]{1,0:T(8,128)S(1)}, u32[]{:S(2)}, u32[]{:S(2)}) %collective-permute-start.1) | collective-permute-done | bytes 8224 | tf_op jit(solution)/shard_map/ppermute | solution.py:16
  174.4 6.0 %fusion.188 = f32[128,1024]{1,0:T(8,128)S(1)} fusion(f32[128,1024]{1,0:T(8,128)S(1)} %convolution_subtract_fusion, f32[128,16]{1,0:T(8,128)S(1)} %collective-permute-done.1, f32[128,16]{1,0:T(8,128)S(1)} %collective-permute-done, f32[1024]{0:T(1024)S(1)} %get-tuple-element.321, f32[1024]{0:T(1024)S(1)} %get-tuple-element.319, ...), kind=kLoop, calls=%fused_computation.371 | loop fusion | flops 12713984 | bytes 1200128 | tf_op jit(solution)/shard_map/add | solution.py:46
  180.4 0.1 fusion.299
  180.5 1.9 collective-permute-start.2
  182.4 4.2 %collective-permute-start.3 = (f32[128,16]{1,0:T(8,128)S(1)}, f32[128,16]{1,0:T(8,128)S(1)}, u32[]{:S(2)}, u32[]{:S(2)}) collective-permute-start(f32[128,16]{1,0:T(8,128)S(1)} %get-tuple-element.104), channel_id=1, source_target_pairs={{1,0},{2,1},{3,2},{4,3},{5,4},{6,5},{7,6},{8,7},{9,8},{10,9},{11,1... | collective-permute-start | bytes 24584 | tf_op jit(solution)/shard_map/ppermute | solution.py:16
  186.6 1.4 collective-permute-done.3
  188.0 6.0 %fusion.96 = f32[128,1024]{1,0:T(8,128)S(1)} fusion(f32[128,1024]{1,0:T(8,128)S(1)} %fusion.188, f32[128,16]{1,0:T(8,128)S(1)} %collective-permute-done.3, f32[128,16]{1,0:T(8,128)S(1)} %collective-permute-done.2, f32[1024]{0:T(1024)S(1)} %get-tuple-element.320, f32[1024]{0:T(1024)S(1)} %get-tuple-element.318, f32[1024]{0:T(1024)S(1)} %get-tuple-element.325, ...), kind=kLoop, calls=%fused_computation.279 | loop fusion | flops 12713984 | bytes 1200128 | tf_op jit(solution)/shard_map/add | solution.py:46
  194.0 0.1 fusion.298
  194.1 1.9 collective-permute-start.4
  196.0 8.0 %collective-permute-start.5 = (f32[128,16]{1,0:T(8,128)S(1)}, f32[128,16]{1,0:T(8,128)S(1)}, u32[]{:S(2)}, u32[]{:S(2)}) collective-permute-start(f32[128,16]{1,0:T(8,128)S(1)} %get-tuple-element.102), channel_id=1, source_target_pairs={{1,0},{2,1},{3,2},{4,3},{5,4},{6,5},{7,6},{8,7},{9,8},{10,9},{11,1... | collective-permute-start | bytes 24584 | tf_op jit(solution)/shard_map/ppermute | solution.py:16
  204.0 0.7 collective-permute-done.5
  204.7 7.3 %fusion.296 = (f32[128]{0:T(128)S(1)}, f32[128,1024]{1,0:T(8,128)S(1)}) fusion(f32[128,16]{1,0:T(8,128)S(1)} %collective-permute-done.5, f32[128,1024]{1,0:T(8,128)S(1)} %fusion.96, f32[1024]{0:T(1024)S(1)} %get-tuple-element.256, f32[1024]{0:T(1024)S(1)} %get-tuple-element.206, f32[1024]{0:T(1024)S(1)} %get-tuple-element.208, ...), kind=kLoop, calls=%fused_computation.626 | loop fusion | flops 12844928 | bytes 1200640 | tf_op jit(solution)/shard_map/reduce_sum | solution.py:98
  212.0 43.9 %psum.15 = f32[128]{0:T(128)S(1)} all-reduce(f32[128]{0:T(128)S(1)} %get-tuple-element.35), channel_id=1, replica_groups=mesh['seg'=4,'bin'=8] {'seg','bin'}, use_global_device_ids=true, to_apply=%region_3.4 | all-reduce | flops 128 | bytes 1024 | tf_op jit(solution)/shard_map/psum | solution.py:98
  255.9 0.5 fusion.277
  256.5 0.2 copy.24
  256.7 41.3 %all-gather = f32[4096,1]{0,1:T(1,128)S(1)} all-gather(f32[128,1]{0,1:T(1,128)S(1)} %slice.1309), channel_id=2, replica_groups=mesh['seg'=4,'bin'=8] {'seg','bin'}, dimensions={0}, use_global_device_ids=true | all-gather | bytes 16896 | tf_op jit(solution)/shard_map/all_gather | solution.py:23
  298.1 0.6 while.10
  298.7 0.9 add_multiply_fusion
  299.6 0.7 copy.44
  (62 shorter events, 0.7 us)
Async XLA Ops:
  7.2 32.0 %copy-start = (f32[256,1024]{1,0:T(8,128)S(1)}, f32[256,1024]{1,0:T(8,128)}, u32[]{:S(2)}) copy-start(f32[256,1024]{1,0:T(8,128)} %param.13) | copy-start | bytes 3145732
  8.6 16.4 %all-to-all-start.1 = ((bf16[8,1,1]{2,1,0:T(2,128)(2,1)}), bf16[8,1,1]{2,1,0:T(2,128)(2,1)S(1)}, u32[]{:S(2)}, u32[]{:S(2)}) async-start(bf16[8,1,1]{2,1,0:T(2,128)(2,1)} %copy.21), calls=%async_computation.1 | async-start | bytes 8192 | tf_op jit(solution)/shard_map/all_to_all | solution.py:68
  17.8 5.9 %copy-start.3 = (bf16[8,128,128]{2,1,0:T(8,128)(2,1)S(1)}, bf16[8,128,128]{2,1,0:T(8,128)(2,1)}, u32[]{:S(2)}) copy-start(bf16[8,128,128]{2,1,0:T(8,128)(2,1)} %param.9) | copy-start | bytes 786436
  22.2 0.7 copy-start.5
  22.9 0.7 copy-start.6
  25.1 13.8 %all-to-all-start = ((bf16[8,128,128]{2,1,0:T(8,128)(2,1)}), bf16[8,128,128]{2,1,0:T(8,128)(2,1)S(1)}, u32[]{:S(2)}, u32[]{:S(2)}) async-start(bf16[8,128,128]{2,1,0:T(8,128)(2,1)} %broadcast_multiply_fusion), calls=%async_computation | async-start | bytes 524288 | tf_op jit(solution)/shard_map/all_to_all | solution.py:67
  30.2 132.4 %all-reduce.2.cloned.1.call-start = ((), (), s32[]{:S(2)}) async-start(), calls=%async_computation.2 | async-start | bytes 262144 | tf_op jit(solution)/shard_map/psum | solution.py:84
  38.9 0.7 copy-start.4
  164.3 6.3 %collective-permute-start = (f32[128,16]{1,0:T(8,128)S(1)}, f32[128,16]{1,0:T(8,128)S(1)}, u32[]{:S(2)}, u32[]{:S(2)}) collective-permute-start(f32[128,16]{1,0:T(8,128)S(1)} %get-tuple-element.105), channel_id=1, source_target_pairs={{0,1},{1,2},{2,3},{3,4},{4,5},{5,6},{6,7},{7,8},{8,9},{9,10},{10,1... | collective-permute-start | bytes 24584 | tf_op jit(solution)/shard_map/ppermute | solution.py:13
  168.6 5.8 %collective-permute-start.1 = (f32[128,16]{1,0:T(8,128)S(1)}, f32[128,16]{1,0:T(8,128)S(1)}, u32[]{:S(2)}, u32[]{:S(2)}) collective-permute-start(f32[128,16]{1,0:T(8,128)S(1)} %get-tuple-element.106), channel_id=1, source_target_pairs={{1,0},{2,1},{3,2},{4,3},{5,4},{6,5},{7,6},{8,7},{9,8},{10,9},{11,1... | collective-permute-start | bytes 24584 | tf_op jit(solution)/shard_map/ppermute | solution.py:16
  180.5 6.1 %collective-permute-start.2 = (f32[128,16]{1,0:T(8,128)S(1)}, f32[128,16]{1,0:T(8,128)S(1)}, u32[]{:S(2)}, u32[]{:S(2)}) collective-permute-start(f32[128,16]{1,0:T(8,128)S(1)} %get-tuple-element.103), channel_id=1, source_target_pairs={{0,1},{1,2},{2,3},{3,4},{4,5},{5,6},{6,7},{7,8},{8,9},{9,10},{10,1... | collective-permute-start | bytes 24584 | tf_op jit(solution)/shard_map/ppermute | solution.py:13
  182.4 5.6 %collective-permute-start.3 = (f32[128,16]{1,0:T(8,128)S(1)}, f32[128,16]{1,0:T(8,128)S(1)}, u32[]{:S(2)}, u32[]{:S(2)}) collective-permute-start(f32[128,16]{1,0:T(8,128)S(1)} %get-tuple-element.104), channel_id=1, source_target_pairs={{1,0},{2,1},{3,2},{4,3},{5,4},{6,5},{7,6},{8,7},{9,8},{10,9},{11,1... | collective-permute-start | bytes 24584 | tf_op jit(solution)/shard_map/ppermute | solution.py:16
  194.1 9.9 %collective-permute-start.4 = (f32[128,16]{1,0:T(8,128)S(1)}, f32[128,16]{1,0:T(8,128)S(1)}, u32[]{:S(2)}, u32[]{:S(2)}) collective-permute-start(f32[128,16]{1,0:T(8,128)S(1)} %get-tuple-element.101), channel_id=1, source_target_pairs={{0,1},{1,2},{2,3},{3,4},{4,5},{5,6},{6,7},{7,8},{8,9},{9,10},{10,1... | collective-permute-start | bytes 24584 | tf_op jit(solution)/shard_map/ppermute | solution.py:13
  196.0 8.7 %collective-permute-start.5 = (f32[128,16]{1,0:T(8,128)S(1)}, f32[128,16]{1,0:T(8,128)S(1)}, u32[]{:S(2)}, u32[]{:S(2)}) collective-permute-start(f32[128,16]{1,0:T(8,128)S(1)} %get-tuple-element.102), channel_id=1, source_target_pairs={{1,0},{2,1},{3,2},{4,3},{5,4},{6,5},{7,6},{8,7},{9,8},{10,9},{11,1... | collective-permute-start | bytes 24584 | tf_op jit(solution)/shard_map/ppermute | solution.py:16
  212.0 44.4 %copy-start.1 = (f32[128,1024]{1,0:T(8,128)}, f32[128,1024]{1,0:T(8,128)S(1)}, u32[]{:S(2)}) copy-start(f32[128,1024]{1,0:T(8,128)S(1)} %get-tuple-element.402) | copy-start | bytes 1572868
  298.7 0.9 copy-start.2
Sparse Core Ops, SparseCore 0:
  41.6 120.9 all-reduce.1
where the time goes:
time: 308 us; the launch traced here: 307 us
  waiting for transfers between devices  136 us (44%)
  blocking collectives  85.2 us (28%)
  starting transfers between devices  32.9 us (11%)
  other arithmetic  22.9 us (7%)
  between operations  14.4 us (5%)
  local copies, waits for them, and re-layouts  11.5 us (4%)
  matrix products  4.3 us (1%)
    psum x1, waiting for transfers between devices, per_device(): coefficients = lax.psum(partial_terms, ('seg', 'bin'))  121 us
    psum x1, blocking collectives, per_device(): totals = lax.psum(jnp.sum(smoothed, axis=1), ('seg', 'bin'))  43.9 us
    all_gather x1, blocking collectives, prefix(): gathered = lax.all_gather(part, axis)  41.3 us
    ppermute x3, starting transfers between devices, extended(): lax.ppermute(lax.slice_in_dim(block, 0, width, axis=dim), axis, backward)  14.1 us
    add x2, other arithmetic, smooth_once(): result + weight[None, :] * padded[:, tap_index:tap_index + out_width]  12 us
    all_to_all x1, waiting for transfers between devices, per_device(): lax.all_to_all(masked, 'bin', split_axis=0, concat_axis=0, tiled=True)  8.52 us
    ppermute x3, starting transfers between devices, extended(): lax.ppermute(lax.slice_in_dim(block, block.shape[dim] - width, None, axis...  8.15 us
    slice x6, local copies, waits for them, and re-layouts, smooth_once(): tap_weights[tap_index]  7.96 us
  transfers between devices with their start and end apart: 9, of which 5 were waited for; matrix products, arithmetic and copies ran while one was open for 3% of the time, Pallas kernels for 0%

commit v1 on v0

--- a/solution.py
+++ b/solution.py
@@ -95,7 +95,7 @@
     for layer_index in range(layers):
         padded = extended(smoothed, ((("seg", "bin"), 1),), half_taps)
         smoothed = smooth_once(padded, kernels[layer_index], labels, bin_dev)
-    totals = lax.psum(jnp.sum(smoothed, axis=1), ("seg", "bin"))
+    totals = jnp.sum(lax.all_gather(jnp.sum(smoothed, axis=1), ("seg", "bin")), axis=0)
     centred = smoothed - (totals / total_bins)[:, None]
     blocks_view = centred.reshape(samples, blocks_dev, block_bins)
     upper_ones = (

time: 308 us -> 304 us (0.987)
  blocking collectives: 85.2 us -> 80.6 us
    psum x1 -> x0, blocking collectives: 43.9 us -> none  [per_device(): totals = lax.psum(jnp.sum(smoothed, axis=1), ('seg', 'bin'))]
    all_gather x0 -> x1, blocking collectives: none -> 42.7 us  [per_device(): lax.all_gather(jnp.sum(smoothed, axis=1), ('seg', 'bin'))]
    all_gather x1, blocking collectives: 41.3 us -> 37.9 us  [prefix(): gathered = lax.all_gather(part, axis)]
    reduce_sum x1 -> x2, other arithmetic: 7.3 us -> 7.35 us  [the longest x1 7.3 us: per_device(): jnp.sum(smoothed, axis=1)]
where the time goes in v1:
time: 304 us; the launch traced here: 303 us
  waiting for transfers between devices  136 us (45%)
  blocking collectives  80.6 us (27%)
  starting transfers between devices  32.9 us (11%)
  other arithmetic  23 us (8%)
  between operations  14.4 us (5%)
  local copies, waits for them, and re-layouts  11.5 us (4%)
  matrix products  4.3 us (1%)
    psum x1, waiting for transfers between devices, per_device(): coefficients = lax.psum(partial_terms, ('seg', 'bin'))  121 us
    all_gather x1, blocking collectives, per_device(): lax.all_gather(jnp.sum(smoothed, axis=1), ('seg', 'bin'))  42.7 us
    all_gather x1, blocking collectives, prefix(): gathered = lax.all_gather(part, axis)  37.9 us
    ppermute x3, starting transfers between devices, extended(): lax.ppermute(lax.slice_in_dim(block, 0, width, axis=dim), axis, backward)  14.1 us
    add x2, other arithmetic, smooth_once(): result + weight[None, :] * padded[:, tap_index:tap_index + out_width]  12 us
    all_to_all x1, waiting for transfers between devices, per_device(): lax.all_to_all(masked, 'bin', split_axis=0, concat_axis=0, tiled=True)  8.52 us
    ppermute x3, starting transfers between devices, extended(): lax.ppermute(lax.slice_in_dim(block, block.shape[dim] - width, None, axis...  8.15 us
    slice x6, local copies, waits for them, and re-layouts, smooth_once(): tap_weights[tap_index]  7.96 us
  transfers between devices with their start and end apart: 9, of which 5 were waited for; matrix products, arithmetic and copies ran while one was open for 3% of the time, Pallas kernels for 0%

profile of v1, /device:TPU:5, one launch (start us, length us, event | category | flops | bytes accessed | tf_op | source)
XLA Modules:
  0.0 302.5 jit_solution(8277347619195395829)
XLA Ops:
  7.2 0.7 convert_bitcast_fusion
  7.9 0.7 copy.21
  8.6 5.5 %all-to-all-start.1 = ((bf16[8,1,1]{2,1,0:T(2,128)(2,1)}), bf16[8,1,1]{2,1,0:T(2,128)(2,1)S(1)}, u32[]{:S(2)}, u32[]{:S(2)}) async-start(bf16[8,1,1]{2,1,0:T(2,128)(2,1)} %copy.21), calls=%async_computation.1 | async-start | bytes 8192 | tf_op jit(solution)/shard_map/all_to_all | solution.py:68
  14.2 0.8 fusion.306
  15.0 1.4 fusion.303
  16.4 1.4 fusion.305
  17.8 1.4 fusion.302
  19.1 1.4 fusion.301
  20.5 1.7 fusion.304
  22.2 0.6 copy-done.5
  22.9 0.6 copy-done.6
  23.6 0.1 convert_reduce_fusion
  23.7 0.7 broadcast_multiply_fusion
  24.5 0.1 broadcast_select_fusion.27
  24.6 0.1 broadcast_select_fusion.95
  24.6 0.1 broadcast_select_fusion.28
  24.8 0.1 broadcast_select_fusion.30
  24.8 0.1 broadcast_select_fusion.29
  25.1 5.1 %all-to-all-start = ((bf16[8,128,128]{2,1,0:T(8,128)(2,1)}), bf16[8,128,128]{2,1,0:T(8,128)(2,1)S(1)}, u32[]{:S(2)}, u32[]{:S(2)}) async-start(bf16[8,128,128]{2,1,0:T(8,128)(2,1)} %broadcast_multiply_fusion), calls=%async_computation | async-start | bytes 524288 | tf_op jit(solution)/shard_map/all_to_all | solution.py:67
  30.2 0.1 reduce.1
  30.4 8.5 %all-to-all-done = bf16[8,128,128]{2,1,0:T(8,128)(2,1)S(1)} async-done(((bf16[8,128,128]{2,1,0:T(8,128)(2,1)}), bf16[8,128,128]{2,1,0:T(8,128)(2,1)S(1)}, u32[]{:S(2)}, u32[]{:S(2)}) %all-to-all-start) | async-done | bytes 262176 | tf_op jit(solution)/shard_map/all_to_all | solution.py:67
  38.9 0.3 fusion
  39.2 0.4 copy-done.4
  39.6 1.8 fusion.286
  41.5 121.1 %all-reduce.2.cloned.1.call-done = f32[128,256]{1,0:T(8,128)} async-done(((f32[128,256]{1,0:T(8,128)}), f32[128,256]{1,0:T(8,128)}) %all-reduce.2.cloned.1.call-update) | async-done | bytes 131088 | tf_op jit(solution)/shard_map/psum | solution.py:84
  162.5 1.7 convolution_subtract_fusion
  164.2 0.1 fusion.300
  164.3 4.3 %collective-permute-start = (f32[128,16]{1,0:T(8,128)S(1)}, f32[128,16]{1,0:T(8,128)S(1)}, u32[]{:S(2)}, u32[]{:S(2)}) collective-permute-start(f32[128,16]{1,0:T(8,128)S(1)} %get-tuple-element.105), channel_id=1, source_target_pairs={{0,1},{1,2},{2,3},{3,4},{4,5},{5,6},{6,7},{7,8},{8,9},{9,10},{10,1... | collective-permute-start | bytes 24584 | tf_op jit(solution)/shard_map/ppermute | solution.py:13
  168.6 1.9 collective-permute-start.1
  170.6 3.9 %collective-permute-done.1 = f32[128,16]{1,0:T(8,128)S(1)} collective-permute-done((f32[128,16]{1,0:T(8,128)S(1)}, f32[128,16]{1,0:T(8,128)S(1)}, u32[]{:S(2)}, u32[]{:S(2)}) %collective-permute-start.1) | collective-permute-done | bytes 8224 | tf_op jit(solution)/shard_map/ppermute | solution.py:16
  174.4 6.0 %fusion.188 = f32[128,1024]{1,0:T(8,128)S(1)} fusion(f32[128,1024]{1,0:T(8,128)S(1)} %convolution_subtract_fusion, f32[128,16]{1,0:T(8,128)S(1)} %collective-permute-done.1, f32[128,16]{1,0:T(8,128)S(1)} %collective-permute-done, f32[1024]{0:T(1024)S(1)} %get-tuple-element.321, f32[1024]{0:T(1024)S(1)} %get-tuple-element.319, ...), kind=kLoop, calls=%fused_computation.371 | loop fusion | flops 12713984 | bytes 1200128 | tf_op jit(solution)/shard_map/add | solution.py:46
  180.4 0.1 fusion.299
  180.5 1.9 collective-permute-start.2
  182.4 4.2 %collective-permute-start.3 = (f32[128,16]{1,0:T(8,128)S(1)}, f32[128,16]{1,0:T(8,128)S(1)}, u32[]{:S(2)}, u32[]{:S(2)}) collective-permute-start(f32[128,16]{1,0:T(8,128)S(1)} %get-tuple-element.104), channel_id=1, source_target_pairs={{1,0},{2,1},{3,2},{4,3},{5,4},{6,5},{7,6},{8,7},{9,8},{10,9},{11,1... | collective-permute-start | bytes 24584 | tf_op jit(solution)/shard_map/ppermute | solution.py:16
  186.6 1.4 collective-permute-done.3
  188.0 6.0 %fusion.96 = f32[128,1024]{1,0:T(8,128)S(1)} fusion(f32[128,1024]{1,0:T(8,128)S(1)} %fusion.188, f32[128,16]{1,0:T(8,128)S(1)} %collective-permute-done.3, f32[128,16]{1,0:T(8,128)S(1)} %collective-permute-done.2, f32[1024]{0:T(1024)S(1)} %get-tuple-element.320, f32[1024]{0:T(1024)S(1)} %get-tuple-element.318, f32[1024]{0:T(1024)S(1)} %get-tuple-element.325, ...), kind=kLoop, calls=%fused_computation.279 | loop fusion | flops 12713984 | bytes 1200128 | tf_op jit(solution)/shard_map/add | solution.py:46
  194.0 0.1 fusion.298
  194.1 1.9 collective-permute-start.4
  196.0 8.0 %collective-permute-start.5 = (f32[128,16]{1,0:T(8,128)S(1)}, f32[128,16]{1,0:T(8,128)S(1)}, u32[]{:S(2)}, u32[]{:S(2)}) collective-permute-start(f32[128,16]{1,0:T(8,128)S(1)} %get-tuple-element.102), channel_id=1, source_target_pairs={{1,0},{2,1},{3,2},{4,3},{5,4},{6,5},{7,6},{8,7},{9,8},{10,9},{11,1... | collective-permute-start | bytes 24584 | tf_op jit(solution)/shard_map/ppermute | solution.py:16
  204.0 0.7 collective-permute-done.5
  204.7 7.3 %fusion.296 = (f32[128]{0:T(128)S(1)}, f32[128,1024]{1,0:T(8,128)S(1)}) fusion(f32[128,16]{1,0:T(8,128)S(1)} %collective-permute-done.5, f32[128,1024]{1,0:T(8,128)S(1)} %fusion.96, f32[1024]{0:T(1024)S(1)} %get-tuple-element.256, f32[1024]{0:T(1024)S(1)} %get-tuple-element.206, f32[1024]{0:T(1024)S(1)} %get-tuple-element.208, ...), kind=kLoop, calls=%fused_computation.626 | loop fusion | flops 12844928 | bytes 1200640 | tf_op jit(solution)/shard_map/reduce_sum | solution.py:98
  212.0 42.7 %all-gather.2 = f32[32,1,128]{2,1,0:T(1,128)S(1)} all-gather(f32[1,1,128]{2,1,0:T(1,128)S(1)} %bitcast.240), channel_id=2, replica_groups=mesh['seg'=4,'bin'=8] {'seg','bin'}, dimensions={0}, use_global_device_ids=true | all-gather | bytes 16896 | tf_op jit(solution)/shard_map/all_gather | solution.py:98
  254.8 0.5 fusion.277
  255.4 0.2 copy.24
  255.6 37.9 %all-gather.1 = f32[4096,1]{0,1:T(1,128)S(1)} all-gather(f32[128,1]{0,1:T(1,128)S(1)} %slice.1309), channel_id=3, replica_groups=mesh['seg'=4,'bin'=8] {'seg','bin'}, dimensions={0}, use_global_device_ids=true | all-gather | bytes 16896 | tf_op jit(solution)/shard_map/all_gather | solution.py:23
  293.5 0.6 while.10
  294.1 0.9 add_multiply_fusion
  295.0 0.7 copy.44
  (63 shorter events, 0.8 us)
Async XLA Ops:
  7.2 32.0 %copy-start = (f32[256,1024]{1,0:T(8,128)S(1)}, f32[256,1024]{1,0:T(8,128)}, u32[]{:S(2)}) copy-start(f32[256,1024]{1,0:T(8,128)} %param.13) | copy-start | bytes 3145732
  8.6 16.4 %all-to-all-start.1 = ((bf16[8,1,1]{2,1,0:T(2,128)(2,1)}), bf16[8,1,1]{2,1,0:T(2,128)(2,1)S(1)}, u32[]{:S(2)}, u32[]{:S(2)}) async-start(bf16[8,1,1]{2,1,0:T(2,128)(2,1)} %copy.21), calls=%async_computation.1 | async-start | bytes 8192 | tf_op jit(solution)/shard_map/all_to_all | solution.py:68
  17.8 5.9 %copy-start.3 = (bf16[8,128,128]{2,1,0:T(8,128)(2,1)S(1)}, bf16[8,128,128]{2,1,0:T(8,128)(2,1)}, u32[]{:S(2)}) copy-start(bf16[8,128,128]{2,1,0:T(8,128)(2,1)} %param.9) | copy-start | bytes 786436
  22.2 0.7 copy-start.5
  22.9 0.7 copy-start.6
  25.1 13.8 %all-to-all-start = ((bf16[8,128,128]{2,1,0:T(8,128)(2,1)}), bf16[8,128,128]{2,1,0:T(8,128)(2,1)S(1)}, u32[]{:S(2)}, u32[]{:S(2)}) async-start(bf16[8,128,128]{2,1,0:T(8,128)(2,1)} %broadcast_multiply_fusion), calls=%async_computation | async-start | bytes 524288 | tf_op jit(solution)/shard_map/all_to_all | solution.py:67
  30.2 132.4 %all-reduce.2.cloned.1.call-start = ((), (), s32[]{:S(2)}) async-start(), calls=%async_computation.2 | async-start | bytes 262144 | tf_op jit(solution)/shard_map/psum | solution.py:84
  38.9 0.7 copy-start.4
  164.3 6.3 %collective-permute-start = (f32[128,16]{1,0:T(8,128)S(1)}, f32[128,16]{1,0:T(8,128)S(1)}, u32[]{:S(2)}, u32[]{:S(2)}) collective-permute-start(f32[128,16]{1,0:T(8,128)S(1)} %get-tuple-element.105), channel_id=1, source_target_pairs={{0,1},{1,2},{2,3},{3,4},{4,5},{5,6},{6,7},{7,8},{8,9},{9,10},{10,1... | collective-permute-start | bytes 24584 | tf_op jit(solution)/shard_map/ppermute | solution.py:13
  168.6 5.8 %collective-permute-start.1 = (f32[128,16]{1,0:T(8,128)S(1)}, f32[128,16]{1,0:T(8,128)S(1)}, u32[]{:S(2)}, u32[]{:S(2)}) collective-permute-start(f32[128,16]{1,0:T(8,128)S(1)} %get-tuple-element.106), channel_id=1, source_target_pairs={{1,0},{2,1},{3,2},{4,3},{5,4},{6,5},{7,6},{8,7},{9,8},{10,9},{11,1... | collective-permute-start | bytes 24584 | tf_op jit(solution)/shard_map/ppermute | solution.py:16
  180.5 6.1 %collective-permute-start.2 = (f32[128,16]{1,0:T(8,128)S(1)}, f32[128,16]{1,0:T(8,128)S(1)}, u32[]{:S(2)}, u32[]{:S(2)}) collective-permute-start(f32[128,16]{1,0:T(8,128)S(1)} %get-tuple-element.103), channel_id=1, source_target_pairs={{0,1},{1,2},{2,3},{3,4},{4,5},{5,6},{6,7},{7,8},{8,9},{9,10},{10,1... | collective-permute-start | bytes 24584 | tf_op jit(solution)/shard_map/ppermute | solution.py:13
  182.4 5.6 %collective-permute-start.3 = (f32[128,16]{1,0:T(8,128)S(1)}, f32[128,16]{1,0:T(8,128)S(1)}, u32[]{:S(2)}, u32[]{:S(2)}) collective-permute-start(f32[128,16]{1,0:T(8,128)S(1)} %get-tuple-element.104), channel_id=1, source_target_pairs={{1,0},{2,1},{3,2},{4,3},{5,4},{6,5},{7,6},{8,7},{9,8},{10,9},{11,1... | collective-permute-start | bytes 24584 | tf_op jit(solution)/shard_map/ppermute | solution.py:16
  194.1 9.9 %collective-permute-start.4 = (f32[128,16]{1,0:T(8,128)S(1)}, f32[128,16]{1,0:T(8,128)S(1)}, u32[]{:S(2)}, u32[]{:S(2)}) collective-permute-start(f32[128,16]{1,0:T(8,128)S(1)} %get-tuple-element.101), channel_id=1, source_target_pairs={{0,1},{1,2},{2,3},{3,4},{4,5},{5,6},{6,7},{7,8},{8,9},{9,10},{10,1... | collective-permute-start | bytes 24584 | tf_op jit(solution)/shard_map/ppermute | solution.py:13
  196.0 8.7 %collective-permute-start.5 = (f32[128,16]{1,0:T(8,128)S(1)}, f32[128,16]{1,0:T(8,128)S(1)}, u32[]{:S(2)}, u32[]{:S(2)}) collective-permute-start(f32[128,16]{1,0:T(8,128)S(1)} %get-tuple-element.102), channel_id=1, source_target_pairs={{1,0},{2,1},{3,2},{4,3},{5,4},{6,5},{7,6},{8,7},{9,8},{10,9},{11,1... | collective-permute-start | bytes 24584 | tf_op jit(solution)/shard_map/ppermute | solution.py:16
  212.0 43.3 %copy-start.1 = (f32[128,1024]{1,0:T(8,128)}, f32[128,1024]{1,0:T(8,128)S(1)}, u32[]{:S(2)}) copy-start(f32[128,1024]{1,0:T(8,128)S(1)} %get-tuple-element.402) | copy-start | bytes 1572868
  294.1 0.9 copy-start.2
Sparse Core Ops, SparseCore 0:
  41.6 120.9 all-reduce.1
